TPU v7x, 128 devices: a whole 4x4x4 slice. The times are simulated.
128 devices in a mesh: body: 8 (over y, core), blk: 16 (over z, x).
Axes of the slice: x: 4, y: 4, z: 4, core: 2. Of those that a mesh axis runs over, the one named last changes fastest.
Arguments:
- psi_init: float32 [65536, 320], P(('body', 'blk')), may hold values from -6 to 6
- source: float32 [65536, 320], P(('body', 'blk'))
- coupling: bfloat16 [65536, 6, 5, 320], P(('body', 'blk')), may hold values from -0.59765625 to 0.59765625
- diag_inv: bfloat16 [65536, 5, 320], P(('body', 'blk')), as said below
- neighbours: int32 [65536, 6], P(('body', 'blk')), may hold values from 0 to 527, as said below
- seam_perm: int32 [8, 8], P('body'), may hold values from 0 to 7, each once within a row
- fringe_src: int32 [128, 1024], P(('body', 'blk')), may hold values from 0 to 511
- fringe_dst: int32 [128, 1024], P(('body', 'blk')), may hold values from 0 to 511, as said below
- fringe_weight: float32 [128, 1024], P(('body', 'blk')), may hold values from 0.2 to 1
Outputs:
- adjoint: float32 [65536, 320], P(('body', 'blk'))
- residual: float32 [65536, 320], P(('body', 'blk'))
Inputs may be any that keep to these rules, and one draw needn't show every extreme that they name: neighbours[i, m] - 8 - (i mod 512) lies in -8 .. 8. `fringe_dst`: every slot names a receiver block. `diag_inv`: each per-cell 5 x 5 matrix has a positive diagonal.
All inputs are finite; a program needn't handle non-finite values.
Results may differ from a plain program's by a relative error of at most 0.0003.
Values sent between devices are 32-bit elements; how exact they have to be, the bound alone decides.
A program may use at most 128 MiB of HBM per device.

v0:
```python
import math

import jax
import jax.numpy as jnp
from jax import lax
from jax.sharding import PartitionSpec as P

CELLS = 64
VARS = 5
BW = 320
STEPS = 2


step_cfl = 0.5


def extended_2(value, sides, width):
    for axis, dim in sides:
        peers, length = (lax.axis_size(axis), value.shape[dim])
        up = [(i, (i + 1) % peers) for i in range(peers)]
        down = [(j, i) for i, j in up]
        last = lax.slice_in_dim(value, length - width, length, axis=dim)
        first = lax.slice_in_dim(value, 0, width, axis=dim)
        before = lax.ppermute(last, axis, up)
        after = lax.ppermute(first, axis, down)
        value = jnp.concatenate([before, value, after], axis=dim)
    return value


def rotate(block, sign):
    first = block[:, 2 * CELLS : 3 * CELLS]
    second = block[:, 3 * CELLS : 4 * CELLS]
    cosine = math.cos(2.0 * math.pi / 3.0)
    sine = sign * math.sin(2.0 * math.pi / 3.0)
    return jnp.concatenate(
        [
            block[:, : 2 * CELLS],
            cosine * first - sine * second,
            sine * first + cosine * second,
            block[:, 4 * CELLS :],
        ],
        axis=1,
    )


def shards(
    psi_init,
    source,
    coupling,
    diag_inv,
    neighbours,
    seam_perm,
    fringe_src,
    fringe_dst,
    fringe_weight,
):
    blocks = psi_init.shape[0]
    rim = seam_perm.shape[1]
    blk_index = lax.axis_index("blk")
    blk_last = lax.axis_size("blk") - 1
    body_count = lax.axis_size("body")
    blk_count = lax.axis_size("blk")
    total = blocks * body_count * blk_count * BW
    onehot = (seam_perm[0][:, None] == jnp.arange(rim, dtype=jnp.int32)[None, :]).astype(
        jnp.float32
    )
    table = (fringe_dst[0][None, :] == jnp.arange(blocks, dtype=jnp.int32)[:, None]).astype(
        jnp.float32
    ) * fringe_weight[0][None, :]
    donors = fringe_src[0]
    psi = psi_init
    resid = psi
    first_norm = None
    for step in range(STEPS):
        padded = extended_2(psi, (("blk", 0),), rim)
        lower = padded[:rim]
        upper = padded[blocks + rim :]
        seam_lo = rotate(jnp.dot(onehot, lower, precision=lax.Precision.HIGHEST), 1.0)
        seam_hi = rotate(jnp.dot(onehot.T, upper, precision=lax.Precision.HIGHEST), -1.0)
        lower = jnp.where(blk_index == 0, seam_lo, lower)
        upper = jnp.where(blk_index == blk_last, seam_hi, upper)
        extended = jnp.concatenate([lower, psi, upper], axis=0)
        outgoing = psi[donors]
        incoming = lax.all_to_all(
            outgoing, ("body", "blk"), split_axis=0, concat_axis=0, tiled=True
        )
        near = extended[neighbours]
        prod = coupling.astype(jnp.float32) * near[:, :, None, :]
        prod = jnp.sum(prod, axis=1).reshape(blocks, VARS, VARS, CELLS)
        coupled = jnp.sum(prod, axis=2).reshape(blocks, BW)
        fringe = jnp.dot(table, incoming, precision=lax.Precision.HIGHEST)
        resid = source - psi + coupled + fringe
        norm_now = lax.psum(jnp.sum(resid * resid), ("body", "blk")) / total + 1e-06
        if first_norm is None:
            first_norm = norm_now
        cfl = step_cfl * jnp.sqrt(first_norm / norm_now)
        prod = (diag_inv.astype(jnp.float32) * resid[:, None, :]).reshape(blocks, VARS, VARS, CELLS)
        update = jnp.sum(prod, axis=2).reshape(blocks, BW)
        psi = psi + cfl * update
    return (psi, resid)


def solution(mesh):
    return jax.shard_map(
        shards,
        mesh=mesh,
        in_specs=(
            P(("body", "blk"), None),
            P(("body", "blk"), None),
            P(("body", "blk"), None, None, None),
            P(("body", "blk"), None, None),
            P(("body", "blk"), None),
            P("body", None),
            P(("body", "blk"), None),
            P(("body", "blk"), None),
            P(("body", "blk"), None),
        ),
        out_specs=(P(("body", "blk"), None), P(("body", "blk"), None)),
        check_vma=False,
    )
```

profile of v0, /device:TPU:1, one launch (start us, length us, event | category | flops | bytes accessed | tf_op | source)
XLA Modules:
  0.0 276.5 jit_solution(14954403684145609946)
XLA Ops:
  4.1 4.8 %collective-permute-start.1 = (f32[8,320]{1,0:T(8,128)S(1)}, f32[8,320]{1,0:T(8,128)S(1)}, u32[]{:S(2)}, u32[]{:S(2)}) collective-permute-start(f32[8,320]{1,0:T(8,128)S(1)} %get-tuple-element.9), channel_id=1, source_target_pairs={{1,0},{2,1},{3,2},{4,3},{5,4},{6,5},{7,6},{8,7},{9,8},{10,9},{11,1... | collective-permute-start | bytes 30728 | tf_op jit(solution)/shard_map/ppermute | solution.py:25
  9.6 4.8 %gather_fusion.1 = f32[1024,320]{1,0:T(8,128)} fusion(f32[512,320]{1,0:T(8,128)S(1)} %copy.29, s32[1024]{0:T(1024)S(1)} %broadcast_clamp_fusion.1), kind=kCustom, calls=%fused_computation.1 | custom fusion | bytes 2625536 | tf_op jit(solution)/shard_map/gather | solution.py:83
  14.4 7.1 %all-to-all-start = ((f32[128,8,320]{2,1,0:T(8,128)}), f32[128,8,320]{2,1,0:T(8,128)}, u32[]{:S(2)}, u32[]{:S(2)}) async-start(f32[128,8,320]{2,1,0:T(8,128)} %bitcast.7), calls=%async_computation | async-start | bytes 3145728 | tf_op jit(solution)/shard_map/all_to_all | solution.py:84
  22.7 12.6 %gather_fusion = f32[3072,320]{1,0:T(8,128)} fusion(f32[528,320]{1,0:T(8,128)S(1)} %pad_maximum_fusion, s32[3072]{0:T(1024)S(1)} %broadcast_clamp_fusion), kind=kCustom, calls=%fused_computation | custom fusion | bytes 7876608 | tf_op jit(solution)/shard_map/gather | solution.py:87
  35.3 6.5 %reshape.72 = f32[512,6,320]{2,1,0:T(8,128)} reshape(f32[3072,320]{1,0:T(8,128)} %gather_fusion) | data formatting | bytes 7864320 | tf_op jit(solution)/shard_map/gather | solution.py:87
  41.9 5.8 %copy.27 = f32[512,6,320]{0,2,1:T(8,128)} copy(f32[512,6,320]{2,1,0:T(8,128)} %reshape.72) | data formatting | bytes 7864320 | tf_op jit(solution)/shard_map/gather | solution.py:87
  47.7 8.9 %fusion = f32[512,5,320]{0,2,1:T(8,128)} fusion(bf16[512,6,5,320]{0,3,2,1:T(8,128)(2,1)} %param.11, f32[512,6,320]{0,2,1:T(8,128)} %copy.27), kind=kLoop, calls=%fused_computation.6 | loop fusion | flops 13926400 | bytes 17039360 | tf_op jit(solution)/shard_map/reduce_sum | solution.py:89
  56.6 2.5 reduce_sum.73
  60.2 5.4 %multiply_reduce_fusion.1 = (f32[]{:T(128)}, f32[512,320]{0,1:T(8,128)S(1)}) fusion(f32[512,320]{0,1:T(8,128)} %bitcast_add_fusion, f32[128,8,320]{2,1,0:T(8,128)} %all-to-all-done, f32[1024]{0:T(1024)S(1)} %bitcast.44, s32[1024]{0:T(1024)S(1)} %bitcast.46), kind=kOutput, calls=%fused_computation.29 | convolution fusion | flops 2014806016 | bytes 2629636 | tf_op jit(solution)/shard_map/dot_general | solution.py:91
  65.6 67.2 %psum.14 = f32[]{:T(128)} all-reduce(f32[]{:T(128)} %get-tuple-element.22), channel_id=1, replica_groups=mesh['body'=8,'blk'=16] {'body','blk'}, use_global_device_ids=true, to_apply=%region_3.4 | all-reduce | flops 1 | bytes 8 | tf_op jit(solution)/shard_map/psum | solution.py:93
  133.5 3.6 %convert_multiply_fusion.3 = f32[512,5,320]{0,2,1:T(8,128)} fusion(bf16[512,5,320]{0,2,1:T(8,128)(2,1)} %param.12, f32[512,320]{0,1:T(8,128)S(1)} %get-tuple-element.23), kind=kLoop, calls=%fused_computation.9 | loop fusion | flops 1638400 | bytes 5570560 | tf_op jit(solution)/shard_map/mul | solution.py:97
  137.1 2.4 reduce_sum.75
  140.4 4.8 %gather_fusion.3 = f32[1024,320]{1,0:T(8,128)} fusion(f32[512,320]{1,0:T(8,128)S(1)} %add.62, s32[1024]{0:T(1024)S(1)} %broadcast_clamp_fusion.1), kind=kCustom, calls=%fused_computation.3 | custom fusion | bytes 2625536 | tf_op jit(solution)/shard_map/gather | solution.py:83
  145.2 4.8 %collective-permute-start.3 = (f32[8,320]{1,0:T(8,128)S(1)}, f32[8,320]{1,0:T(8,128)S(1)}, u32[]{:S(2)}, u32[]{:S(2)}) collective-permute-start(f32[8,320]{1,0:T(8,128)S(1)} %get-tuple-element.7), channel_id=1, source_target_pairs={{1,0},{2,1},{3,2},{4,3},{5,4},{6,5},{7,6},{8,7},{9,8},{10,9},{11,1... | collective-permute-start | bytes 30728 | tf_op jit(solution)/shard_map/ppermute | solution.py:25
  150.0 5.9 %all-to-all-start.1 = ((f32[128,8,320]{2,1,0:T(8,128)}), f32[128,8,320]{2,1,0:T(8,128)}, u32[]{:S(2)}, u32[]{:S(2)}) async-start(f32[128,8,320]{2,1,0:T(8,128)} %bitcast.39), calls=%async_computation.1 | async-start | bytes 3145728 | tf_op jit(solution)/shard_map/all_to_all | solution.py:84
  156.7 12.6 %gather_fusion.2 = f32[3072,320]{1,0:T(8,128)} fusion(f32[528,320]{1,0:T(8,128)S(1)} %pad_maximum_fusion.1, s32[3072]{0:T(1024)S(1)} %broadcast_clamp_fusion), kind=kCustom, calls=%fused_computation.2 | custom fusion | bytes 7876608 | tf_op jit(solution)/shard_map/gather | solution.py:87
  169.4 6.5 %reshape.88 = f32[512,6,320]{2,1,0:T(8,128)} reshape(f32[3072,320]{1,0:T(8,128)} %gather_fusion.2) | data formatting | bytes 7864320 | tf_op jit(solution)/shard_map/gather | solution.py:87
  175.9 5.8 %copy.32 = f32[512,6,320]{0,2,1:T(8,128)} copy(f32[512,6,320]{2,1,0:T(8,128)} %reshape.88) | data formatting | bytes 7864320 | tf_op jit(solution)/shard_map/gather | solution.py:87
  181.7 8.9 %fusion.1 = f32[512,5,320]{0,2,1:T(8,128)} fusion(bf16[512,6,5,320]{0,3,2,1:T(8,128)(2,1)} %param.11, f32[512,6,320]{0,2,1:T(8,128)} %copy.32), kind=kLoop, calls=%fused_computation.7 | loop fusion | flops 13926400 | bytes 17039360 | tf_op jit(solution)/shard_map/reduce_sum | solution.py:89
  190.6 2.4 reduce_sum.77
  194.1 6.8 %multiply_reduce_fusion = (f32[]{:T(128)}, f32[512,320]{1,0:T(8,128)}) fusion(f32[128,8,320]{2,1,0:T(8,128)} %all-to-all-done.1, f32[1024]{0:T(1024)S(1)} %bitcast.45, s32[1024]{0:T(1024)S(1)} %bitcast.47, f32[512,320]{1,0:T(8,128)} %copy.33, f32[512,320]{1,0:T(8,128)S(1)} %copy.31, f32[512,320]{1,0:T(8,128)S(1)} %add.62), kind=kOutput, calls=%fused_computation.27 | convolution fusion | flops 2015133696 | bytes 3940356 | tf_op jit(solution)/shard_map/dot_general | solution.py:91
  200.9 67.3 %psum.15 = f32[]{:T(128)} all-reduce(f32[]{:T(128)} %get-tuple-element.24), channel_id=1, replica_groups=mesh['body'=8,'blk'=16] {'body','blk'}, use_global_device_ids=true, to_apply=%region_8.9 | all-reduce | flops 1 | bytes 8 | tf_op jit(solution)/shard_map/psum | solution.py:93
  270.4 2.2 convert_multiply_fusion.2
  272.6 2.4 reduce_sum.79
  (62 shorter events, 12.2 us)
Async XLA Ops:
  2.0 19.9 %collective-permute-start = (f32[8,320]{1,0:T(8,128)S(1)}, f32[8,320]{1,0:T(8,128)S(1)}, u32[]{:S(2)}, u32[]{:S(2)}) collective-permute-start(f32[8,320]{1,0:T(8,128)S(1)} %get-tuple-element.8), channel_id=1, source_target_pairs={{0,1},{1,2},{2,3},{3,4},{4,5},{5,6},{6,7},{7,8},{8,9},{9,10},{10,1... | collective-permute-start | bytes 30728 | tf_op jit(solution)/shard_map/ppermute | solution.py:24
  4.1 18.1 %collective-permute-start.1 = (f32[8,320]{1,0:T(8,128)S(1)}, f32[8,320]{1,0:T(8,128)S(1)}, u32[]{:S(2)}, u32[]{:S(2)}) collective-permute-start(f32[8,320]{1,0:T(8,128)S(1)} %get-tuple-element.9), channel_id=1, source_target_pairs={{1,0},{2,1},{3,2},{4,3},{5,4},{6,5},{7,6},{8,7},{9,8},{10,9},{11,1... | collective-permute-start | bytes 30728 | tf_op jit(solution)/shard_map/ppermute | solution.py:25
  9.6 11.9 %copy-start.4 = (s32[512,6]{0,1:T(8,128)S(1)}, s32[512,6]{0,1:T(8,128)}, u32[]{:S(2)}) copy-start(s32[512,6]{0,1:T(8,128)} %param.13) | copy-start | bytes 36868
  14.4 7.5 %copy-start.7 = (s32[1,8]{1,0:T(1,128)S(1)}, s32[1,8]{1,0:T(1,128)}, u32[]{:S(2)}) copy-start(s32[1,8]{1,0:T(1,128)} %param.14) | copy-start | bytes 100
  14.4 45.7 %all-to-all-start = ((f32[128,8,320]{2,1,0:T(8,128)}), f32[128,8,320]{2,1,0:T(8,128)}, u32[]{:S(2)}, u32[]{:S(2)}) async-start(f32[128,8,320]{2,1,0:T(8,128)} %bitcast.7), calls=%async_computation | async-start | bytes 3145728 | tf_op jit(solution)/shard_map/all_to_all | solution.py:84
  56.6 2.5 copy-start.1
  56.6 2.5 copy-start.2
  56.6 3.5 %copy-start.5 = (f32[1,1024]{1,0:T(1,128)S(1)}, f32[1,1024]{1,0:T(1,128)}, u32[]{:S(2)}) copy-start(f32[1,1024]{1,0:T(1,128)} %param.17) | copy-start | bytes 12292
  56.6 3.5 %copy-start.6 = (s32[1,1024]{1,0:T(1,128)S(1)}, s32[1,1024]{1,0:T(1,128)}, u32[]{:S(2)}) copy-start(s32[1,1024]{1,0:T(1,128)} %param.16) | copy-start | bytes 12292
  139.9 16.0 %collective-permute-start.2 = (f32[8,320]{1,0:T(8,128)S(1)}, f32[8,320]{1,0:T(8,128)S(1)}, u32[]{:S(2)}, u32[]{:S(2)}) collective-permute-start(f32[8,320]{1,0:T(8,128)S(1)} %get-tuple-element.6), channel_id=1, source_target_pairs={{0,1},{1,2},{2,3},{3,4},{4,5},{5,6},{6,7},{7,8},{8,9},{9,10},{10,1... | collective-permute-start | bytes 30728 | tf_op jit(solution)/shard_map/ppermute | solution.py:24
  145.2 10.9 %collective-permute-start.3 = (f32[8,320]{1,0:T(8,128)S(1)}, f32[8,320]{1,0:T(8,128)S(1)}, u32[]{:S(2)}, u32[]{:S(2)}) collective-permute-start(f32[8,320]{1,0:T(8,128)S(1)} %get-tuple-element.7), channel_id=1, source_target_pairs={{1,0},{2,1},{3,2},{4,3},{5,4},{6,5},{7,6},{8,7},{9,8},{10,9},{11,1... | collective-permute-start | bytes 30728 | tf_op jit(solution)/shard_map/ppermute | solution.py:25
  150.0 44.1 %all-to-all-start.1 = ((f32[128,8,320]{2,1,0:T(8,128)}), f32[128,8,320]{2,1,0:T(8,128)}, u32[]{:S(2)}, u32[]{:S(2)}) async-start(f32[128,8,320]{2,1,0:T(8,128)} %bitcast.39), calls=%async_computation.1 | async-start | bytes 3145728 | tf_op jit(solution)/shard_map/all_to_all | solution.py:84
  194.1 76.2 %copy-start = (bf16[512,5,320]{0,2,1:T(8,128)(2,1)S(1)}, bf16[512,5,320]{0,2,1:T(8,128)(2,1)}, u32[]{:S(2)}) copy-start(bf16[512,5,320]{0,2,1:T(8,128)(2,1)} %param.12) | copy-start | bytes 4915204
  270.4 2.2 copy-start.3
where the time goes:
time: 277 us; the launch traced here: 276 us
  blocking collectives  134 us (48%)
  local copies, waits for them, and re-layouts  65.7 us (24%)
  other arithmetic  35.9 us (13%)
  starting transfers between devices  24.9 us (9%)
  matrix products  13.1 us (5%)
    psum x2, blocking collectives, shards(): norm_now = lax.psum(jnp.sum(resid * resid), ('body', 'blk')) / total + 1e-06  134 us
    gather x6, local copies, waits for them, and re-layouts, shards(): near = extended[neighbours]  49.9 us
    reduce_sum x2, other arithmetic, shards(): prod = jnp.sum(prod, axis=1).reshape(blocks, VARS, VARS, CELLS)  17.8 us
    all_to_all x2, starting transfers between devices, shards(): lax.all_to_all(outgoing, ('body', 'blk'), split_axis=0, concat_axis=0, ti...  12.9 us
    dot_general x2, matrix products, shards(): fringe = jnp.dot(table, incoming, precision=lax.Precision.HIGHEST)  12.2 us
    gather x2, local copies, waits for them, and re-layouts, shards(): outgoing = psi[donors]  9.59 us
    ppermute x2, starting transfers between devices, extended_2(): after = lax.ppermute(first, axis, down)  9.59 us
    mul x2, other arithmetic, shards(): diag_inv.astype(jnp.float32) * resid[:, None, :]  5.8 us
  transfers between devices with their start and end apart: 6, of which 0 were waited for; matrix products, arithmetic and copies ran while one was open for 32% of the time, Pallas kernels for 0%

commit v1 on v0

v1 whole, which is shorter than its diff:
```python
import math

import jax
import jax.numpy as jnp
from jax import lax
from jax.experimental import pallas as pl
from jax.experimental.pallas import tpu as pltpu
from jax.sharding import PartitionSpec as P

CELLS = 64
VARS = 5
BW = 320
NB = 512
SLOTS = 6
RIM = 8
CAP = 8
BODIES = 8
BLKS = 16
DEVS = 128
CHUNKS = 2
CC = CELLS // CHUNKS
CU = VARS * CC
ROWS = CU * CAP // 128
STEPS = 2
CFL = 0.5
LANES = 128
TILES = NB // LANES
TOTAL = DEVS * NB * BW
MESH = pl.DeviceIdType.MESH
F32 = jnp.float32
BF16 = jnp.bfloat16


def iota(shape, dim):
    return lax.broadcasted_iota(jnp.int32, shape, dim)


def split(x):
    hi = x.astype(BF16)
    return hi, (x - hi.astype(F32)).astype(BF16)


def dot(a, b):
    return jnp.dot(a, b, preferred_element_type=F32)


def dot_t(a, b):
    return lax.dot_general(a, b, (((1,), (1,)), ((), ())), preferred_element_type=F32)


def device(o):
    return (lax.div(o, BLKS), lax.rem(o, BLKS))


def kernel(
    psi_hbm, src_hbm, coup_hbm, dinv_hbm, nbr_hbm, perm, fsrc_hbm, fdst_hbm, fw_hbm,
    adj_hbm, res_hbm,
    psi, src, coup, dinv, nbr, fsrc, fdst, fw,
    sel, tab, near_hot, const, rim_hot,
    halves, halo, near, base, fringe, inc_t, prec,
    out, inc, sums, total,
    lsem, ssem, rsem, rim_ssem, rim_rsem, sum_ssem, sum_rsem,
):
    b, k = lax.axis_index("body"), lax.axis_index("blk")
    me = b * BLKS + k
    nxt, prv = lax.rem(k + 1, BLKS), lax.rem(k + BLKS - 1, BLKS)

    loads = [
        pltpu.make_async_copy(s, d, lsem.at[i])
        for i, (s, d) in enumerate(
            [(psi_hbm, psi), (fsrc_hbm, fsrc), (nbr_hbm, nbr), (fdst_hbm, fdst), (fw_hbm, fw),
             (src_hbm, src), (dinv_hbm, dinv), (coup_hbm, coup)]
        )
    ]
    for c in loads:
        c.start()

    bar = pltpu.get_barrier_semaphore()

    def greet(i, carry):
        o = lax.rem(me + i, DEVS)
        pl.semaphore_signal(bar, inc=1, device_id=device(o), device_id_type=MESH)
        return carry

    lax.fori_loop(1, DEVS, greet, 0)

    def slab(ref, s, c, first, count):
        return ref.at[s, c, pl.ds(first, count), pl.ds(0, ROWS)]

    def halve(c):
        for v in range(VARS):
            hi, lo = split(psi[v * CELLS + c * CC : v * CELLS + (c + 1) * CC, :])
            halves[c, 0, v * CC : (v + 1) * CC, :] = hi
            halves[c, 1, v * CC : (v + 1) * CC, :] = lo

    def pack(y):
        n = y.shape[1]
        main = y[:LANES].T.reshape(n // CAP, CAP, LANES)
        rem = y[LANES:]
        parts = [rem] + [pltpu.roll(rem, n - 2 * g, 1) for g in range(1, 4)]
        rest = jnp.concatenate(parts, axis=0).T.reshape(n // CAP, CAP, LANES)
        return main, rest

    def unpack(main, rest):
        n = main.shape[0] * CAP
        top = main.reshape(n, LANES).T
        x = rest.reshape(n, LANES).T
        group = lax.rem(iota((CC, n), 1), CAP) // 2
        low = x[:CC]
        for g in range(1, 4):
            low = jnp.where(group == g, pltpu.roll(x[g * CC : (g + 1) * CC], 2 * g, 1), low)
        return jnp.concatenate([top, low], axis=0)

    def rims(s, c):
        y = dot(halves[c, 0], const[...]) + dot(halves[c, 1], const[...])
        halo[c] = y[:, LANES:]
        main, rest = pack(y[:, :LANES])
        out[s, c, DEVS : DEVS + 2, 0:8] = main[:2]
        out[s, c, DEVS : DEVS + 2, 8:16] = rest[:2]

    def rim_copies(s, c):
        return [
            pltpu.make_async_remote_copy(
                slab(out, s, c, DEVS + i, 1), slab(inc, s, c, DEVS + i, 1),
                rim_ssem.at[s, c, i], rim_rsem.at[s, c, i],
                device_id=(b, to), device_id_type=MESH,
            )
            for i, to in enumerate((nxt, prv))
        ]

    def donors(s, c):
        def block(t, carry):
            cols = pl.ds(pl.multiple_of(t * 256, 256), 256)
            y = dot(halves[c, 0], sel[:, cols]) + dot(halves[c, 1], sel[:, cols])
            main, rest = pack(y)
            out[s, c, pl.ds(t * 32, 32), 0:8] = main
            out[s, c, pl.ds(t * 32, 32), 8:16] = rest
            return carry

        lax.fori_loop(0, 4, block, 0)
        inc[s, c, pl.ds(me, 1)] = out[s, c, pl.ds(me, 1)]

    def send(s, c):
        for r in rim_copies(s, c):
            r.start()

        def one(i, carry):
            o = lax.rem(me + lax.rem(i * 37, DEVS), DEVS)
            pltpu.make_async_remote_copy(
                slab(out, s, c, o, 1), slab(inc, s, c, me, 1), ssem.at[s, c], rsem.at[s, c],
                device_id=device(o), device_id_type=MESH,
            ).start()
            return carry

        lax.fori_loop(1, DEVS, one, 0)

    def wait_rims(s, c):
        for r in rim_copies(s, c):
            r.wait_recv()

    def wait_fringe(s, c):
        ref = slab(inc, s, c, 0, DEVS - 1)
        pltpu.make_async_copy(ref, ref, rsem.at[s, c]).wait()

    def wait_sends(s, c):
        ref = slab(out, s, c, 0, DEVS - 1)
        pltpu.make_async_copy(ref, ref, ssem.at[s, c]).wait()
        for r in rim_copies(s, c):
            r.wait_send()

    def couple(s, c):
        wait_rims(s, c)
        zero = jnp.zeros((14, CAP, LANES), F32)
        main = jnp.concatenate([inc[s, c, DEVS : DEVS + 2, 0:8], zero], axis=0)
        rest = jnp.concatenate([inc[s, c, DEVS : DEVS + 2, 8:16], zero], axis=0)
        hi, lo = split(unpack(main, rest))
        edge = halo[c] + (dot(hi, rim_hot[...]) + dot(lo, rim_hot[...]))
        lane = iota((1, LANES), 1)
        turn_lo = (lane < RIM) & (k == 0)
        turn_hi = (lane >= 56) & (lane < 64) & (k == BLKS - 1)
        cosine = jnp.where(turn_lo | turn_hi, math.cos(2.0 * math.pi / 3.0), 1.0)
        sine = math.sin(2.0 * math.pi / 3.0)
        sine = jnp.where(turn_lo, sine, jnp.where(turn_hi, -sine, 0.0))
        e2, e3 = edge[2 * CC : 3 * CC], edge[3 * CC : 4 * CC]
        edge = jnp.concatenate(
            [edge[: 2 * CC], cosine * e2 - sine * e3, sine * e2 + cosine * e3, edge[4 * CC :]], axis=0
        )
        ehi, elo = split(edge)

        def tile(t, carry):
            cols = pl.ds(pl.multiple_of(t * LANES, LANES), LANES)
            ahi = jnp.concatenate([halves[c, 0, :, cols], ehi], axis=1)
            alo = jnp.concatenate([halves[c, 1, :, cols], elo], axis=1)
            near[...] = dot(ahi, near_hot[t]) + dot(alo, near_hot[t])
            acc = jnp.zeros((VARS, CC, LANES), F32)
            for v in range(VARS):
                rows = slice(v * CELLS + c * CC, v * CELLS + (c + 1) * CC)
                for m in range(SLOTS):
                    x = near[v * CC : (v + 1) * CC, m * LANES : (m + 1) * LANES]
                    acc = acc + coup[m, :, rows, cols].astype(F32) * x[None]
            for v in range(VARS):
                rows = slice(v * CELLS + c * CC, v * CELLS + (c + 1) * CC)
                base[c, v * CC : (v + 1) * CC, cols] = src[rows, cols] - psi[rows, cols] + acc[v]
            return carry

        lax.fori_loop(0, TILES, tile, 0)

    def gather_fringe(s, c):
        wait_fringe(s, c)

        def block(t, carry):
            cols = pl.ds(pl.multiple_of(t * 256, 256), 256)
            x = unpack(inc[s, c, pl.ds(t * 32, 32), 0:8], inc[s, c, pl.ds(t * 32, 32), 8:16])
            hi, lo = split(x * fw[:, cols])
            inc_t[0, :, cols] = hi
            inc_t[1, :, cols] = lo
            return carry

        lax.fori_loop(0, 4, block, 0)
        fringe[...] = dot_t(inc_t[0], tab[...]) + dot_t(inc_t[1], tab[...])

    def residual(s, c, square):
        def tile(t, square):
            cols = pl.ds(pl.multiple_of(t * LANES, LANES), LANES)
            acc = jnp.zeros((VARS, CC, LANES), F32)
            for v in range(VARS):
                rows = slice(v * CELLS + c * CC, v * CELLS + (c + 1) * CC)
                own = slice(v * CC, (v + 1) * CC)
                r = base[c, own, cols] + fringe[own, cols]
                square = square + jnp.sum((r * r).reshape(CC // 8, 8, LANES), axis=0)
                acc = acc + dinv[:, rows, cols].astype(F32) * r[None]
                if s == STEPS - 1:
                    src[rows, cols] = r
            for v in range(VARS):
                rows = slice(v * CELLS + c * CC, v * CELLS + (c + 1) * CC)
                if s == STEPS - 1:
                    prec[rows, cols] = acc[v]
                else:
                    psi[rows, cols] = psi[rows, cols] + CFL * acc[v]
            return square

        return lax.fori_loop(0, TILES, tile, square)

    loads[0].wait()
    loads[1].wait()
    halve(0)
    tgt = iota((1, 2 * LANES), 1)
    h = tgt - LANES
    t, e = h // 16, lax.rem(h, 16)
    own = jnp.where(e < RIM, LANES * t - RIM + e, LANES * (t + 1) + e - RIM)
    own = jnp.where(h < 64, own, -1)
    rim = jnp.where(tgt < RIM, NB - RIM + tgt, jnp.where(tgt < 2 * RIM, tgt - RIM, -1))
    tgt = jnp.where(tgt < LANES, rim, own)

    def build(i, carry):
        at = pl.multiple_of(i * 64, 64)
        row = iota((64, DEVS * CAP), 0) + at
        sel[pl.ds(at, 64)] = jnp.where(row == fsrc[...], 1.0, 0.0).astype(BF16)
        const[pl.ds(at, 64)] = jnp.where(row[:, : 2 * LANES] == tgt, 1.0, 0.0).astype(BF16)
        return carry

    lax.fori_loop(0, NB // 64, build, 0)
    rims(0, 0)
    donors(0, 0)
    pl.semaphore_wait(bar, DEVS - 1)
    send(0, 0)
    for c in range(1, CHUNKS):
        halve(c)
        rims(0, c)
        donors(0, c)
        send(0, c)

    for c in loads[2:5]:
        c.wait()

    def build_in(i, carry):
        at = pl.multiple_of(i * 64, 64)
        row = iota((64, DEVS * CAP), 0) + at
        tab[pl.ds(at, 64)] = jnp.where(row == fdst[...], 1.0, 0.0).astype(BF16)
        return carry

    lax.fori_loop(0, NB // 64, build_in, 0)
    row = iota((2 * LANES, LANES), 0)
    for t in range(TILES):
        for m in range(SLOTS):
            d = nbr[m : m + 1, t * LANES : (t + 1) * LANES] - (RIM + t * LANES)
            d = jnp.where(d < 0, d + (LANES + 16 * t + RIM), jnp.where(d >= LANES, d + (16 * t + RIM), d))
            near_hot[t, :, m * LANES : (m + 1) * LANES] = jnp.where(row == d, 1.0, 0.0).astype(BF16)
    row, col = iota((LANES, LANES), 0), iota((LANES, LANES), 1)
    hot = jnp.zeros((LANES, LANES), F32)
    for j in range(RIM):
        p = perm[0, j]
        low = jnp.where(k == 0, p, j)
        high = jnp.where(k == BLKS - 1, p, j) + 56
        hot = jnp.where((row == low) & (col == j), 1.0, hot)
        hot = jnp.where((row == RIM + j) & (col == high), 1.0, hot)
    rim_hot[...] = hot.astype(BF16)
    for c in loads[5:]:
        c.wait()

    square = [jnp.zeros((8, LANES), F32) for _ in range(STEPS)]
    for s in range(STEPS):
        for c in range(CHUNKS):
            couple(s, c)
        for c in range(CHUNKS):
            gather_fringe(s, c)
            square[s] = residual(s, c, square[s])
            if s < STEPS - 1:
                halve(c)
                rims(s + 1, c)
                donors(s + 1, c)
                send(s + 1, c)

    sums[...] = jnp.concatenate([jnp.sum(x, axis=0, keepdims=True) for x in square], axis=0)[None]
    total[pl.ds(me, 1)] = sums[...]

    def tell(i, carry):
        o = lax.rem(me + i, DEVS)
        pltpu.make_async_remote_copy(
            sums.at[0], total.at[me], sum_ssem, sum_rsem, device_id=device(o), device_id_type=MESH
        ).start()
        return carry

    lax.fori_loop(1, DEVS, tell, 0)
    res = pltpu.make_async_copy(src, res_hbm, lsem.at[0])
    res.start()
    ref = total.at[pl.ds(0, DEVS - 1)]
    pltpu.make_async_copy(ref, ref, sum_rsem).wait()
    q = jnp.sum(jnp.sum(total[...], axis=0), axis=1, keepdims=True) * (1.0 / TOTAL) + 1e-06
    cfl = CFL * jnp.sqrt(q[0:1] / q[1:2])

    def last(i, carry):
        rows = pl.ds(pl.multiple_of(i * 32, 32), 32)
        psi[rows] = psi[rows] + cfl * prec[rows]
        return carry

    lax.fori_loop(0, BW // 32, last, 0)
    adj = pltpu.make_async_copy(psi, adj_hbm, lsem.at[1])
    adj.start()
    pltpu.make_async_copy(ref, ref, sum_ssem).wait()
    for s in range(STEPS):
        for c in range(CHUNKS):
            wait_sends(s, c)
    res.wait()
    adj.wait()


def shards(psi, source, coupling, diag_inv, neighbours, seam_perm, fringe_src, fringe_dst, fringe_weight):
    any_space = pl.BlockSpec(memory_space=pl.ANY)
    vmem = pltpu.VMEM
    dma = pltpu.SemaphoreType.DMA
    slots = DEVS * CAP
    adjoint, residual = pl.pallas_call(
        kernel,
        out_shape=[jax.ShapeDtypeStruct((BW, NB), F32)] * 2,
        in_specs=[any_space] * 5 + [pl.BlockSpec(memory_space=pltpu.SMEM)] + [any_space] * 3,
        out_specs=[any_space] * 2,
        scratch_shapes=[
            vmem((BW, NB), F32),
            vmem((BW, NB), F32),
            vmem((SLOTS, VARS, BW, NB), BF16),
            vmem((VARS, BW, NB), BF16),
            vmem((SLOTS, NB), jnp.int32),
            vmem((1, slots), jnp.int32),
            vmem((1, slots), jnp.int32),
            vmem((1, slots), F32),
            vmem((NB, slots), BF16),
            vmem((NB, slots), BF16),
            vmem((TILES, 2 * LANES, SLOTS * LANES), BF16),
            vmem((NB, 2 * LANES), BF16),
            vmem((LANES, LANES), BF16),
            vmem((CHUNKS, 2, CU, NB), BF16),
            vmem((CHUNKS, CU, LANES), F32),
            vmem((CU, SLOTS * LANES), F32),
            vmem((CHUNKS, CU, NB), F32),
            vmem((CU, NB), F32),
            vmem((2, CU, slots), BF16),
            vmem((BW, NB), F32),
            vmem((STEPS, CHUNKS, DEVS + 2, 16, LANES), F32),
            vmem((STEPS, CHUNKS, DEVS + 2, 16, LANES), F32),
            vmem((1, STEPS, LANES), F32),
            vmem((DEVS, STEPS, LANES), F32),
            dma((8,)),
            dma((STEPS, CHUNKS)),
            dma((STEPS, CHUNKS)),
            dma((STEPS, CHUNKS, 2)),
            dma((STEPS, CHUNKS, 2)),
            dma,
            dma,
        ],
        compiler_params=pltpu.CompilerParams(
            collective_id=0, has_side_effects=True, vmem_limit_bytes=48 << 20
        ),
        name="adjoint_steps",
    )(
        psi.T, source.T, coupling.transpose(1, 2, 3, 0), diag_inv.transpose(1, 2, 0), neighbours.T,
        seam_perm, fringe_src, fringe_dst, fringe_weight,
    )
    return adjoint.T, residual.T


def solution(mesh):
    rows = P(("body", "blk"))
    return jax.shard_map(
        shards,
        mesh=mesh,
        in_specs=(rows, rows, rows, rows, rows, P("body"), rows, rows, rows),
        out_specs=(rows, rows),
        check_vma=False,
    )
```

time: 277 us -> 67 us (0.24)
  blocking collectives: 134 us -> 0 us
  Pallas kernels: 0 us -> 57.2 us
  local copies, waits for them, and re-layouts: 65.7 us -> 8.7 us
  other arithmetic: 35.9 us -> 0 us
  starting transfers between devices: 24.9 us -> 0 us
  matrix products: 13.1 us -> 0 us
    psum x2 -> x0, blocking collectives: 134 us -> none  [shards(): norm_now = lax.psum(jnp.sum(resid * resid), ('body', 'blk')) / total + 1e-06]
    gather x8 -> x0, local copies, waits for them, and re-layouts: 59.5 us -> none  [the longest x6 49.9 us: shards(): near = extended[neighbours]]
    pallas_call x0 -> x1, Pallas kernels: none -> 57.2 us  [shards(): pl.pallas_call(kernel, out_shape=[jax.ShapeDtypeStruct((BW, NB), F32)] *...]
    reduce_sum x6 -> x0, other arithmetic: 27.3 us -> none  [the longest x2 17.8 us: shards(): prod = jnp.sum(prod, axis=1).reshape(blocks, VARS, VARS, CELLS)]
    dot_general x6 -> x0, matrix products: 13.1 us -> none  [the longest x2 12.2 us: shards(): fringe = jnp.dot(table, incoming, precision=lax.Precision.HIGHEST)]
    all_to_all x2 -> x0, starting transfers between devices: 12.9 us -> none  [shards(): lax.all_to_all(outgoing, ('body', 'blk'), split_axis=0, concat_axis=0, ti...]
    ppermute x4 -> x0, starting transfers between devices: 12 us -> none  [the longest x2 9.59 us: extended_2(): after = lax.ppermute(first, axis, down)]
    unnamed x19 -> x18, local copies, waits for them, and re-layouts: 2.74 us -> 8.7 us
  transfers between devices with their start and end apart: 6 -> 0, of which waited for: 0 -> 0; matrix products, arithmetic and copies ran while one was open for 32% -> 0% of each run, Pallas kernels for 0% -> 0%
where the time goes in v1:
time: 67 us; the launch traced here: 66.6 us
  Pallas kernels  57.2 us (85%)
  local copies, waits for them, and re-layouts  8.7 us (13%)
    pallas_call x1, Pallas kernels, shards(): pl.pallas_call(kernel, out_shape=[jax.ShapeDtypeStruct((BW, NB), F32)] *...  57.2 us
    unnamed x18, local copies, waits for them, and re-layouts  8.7 us

profile of v1, /device:TPU:1, one launch (start us, length us, event | category | flops | bytes accessed | tf_op | source)
XLA Modules:
  0.0 66.6 jit_solution(13506432255937083071)
XLA Ops:
  0.6 0.0 copy-start
  0.6 1.4 %copy-done = bf16[512,5,320]{0,2,1:T(8,128)(2,1)S(1)} copy-done((bf16[512,5,320]{0,2,1:T(8,128)(2,1)S(1)}, bf16[512,5,320]{0,2,1:T(8,128)(2,1)}, u32[]{:S(2)}) %copy-start) | copy-done | bytes 1638424
  2.1 0.0 copy-start.1
  2.1 1.1 %copy-done.1 = f32[512,320]{0,1:T(8,128)S(1)} copy-done((f32[512,320]{0,1:T(8,128)S(1)}, f32[512,320]{0,1:T(8,128)}, u32[]{:S(2)}) %copy-start.1) | copy-done | bytes 655384
  3.2 0.0 copy-start.2
  3.2 1.1 %copy-done.2 = f32[512,320]{0,1:T(8,128)S(1)} copy-done((f32[512,320]{0,1:T(8,128)S(1)}, f32[512,320]{0,1:T(8,128)}, u32[]{:S(2)}) %copy-start.2) | copy-done | bytes 655384
  4.2 0.0 copy-start.3
  4.2 0.7 %copy-done.3 = s32[512,6]{0,1:T(8,128)S(1)} copy-done((s32[512,6]{0,1:T(8,128)S(1)}, s32[512,6]{0,1:T(8,128)}, u32[]{:S(2)}) %copy-start.3) | copy-done | bytes 12312
  5.0 0.0 copy-start.4
  5.0 0.7 %copy-done.4 = s32[1,1024]{1,0:T(1,128)S(1)} copy-done((s32[1,1024]{1,0:T(1,128)S(1)}, s32[1,1024]{1,0:T(1,128)}, u32[]{:S(2)}) %copy-start.4) | copy-done | bytes 4120
  5.6 0.0 copy-start.5
  5.6 0.7 %copy-done.5 = s32[1,1024]{1,0:T(1,128)S(1)} copy-done((s32[1,1024]{1,0:T(1,128)S(1)}, s32[1,1024]{1,0:T(1,128)}, u32[]{:S(2)}) %copy-start.5) | copy-done | bytes 4120
  6.3 0.0 copy-start.6
  6.3 0.7 %copy-done.6 = f32[1,1024]{1,0:T(1,128)S(1)} copy-done((f32[1,1024]{1,0:T(1,128)S(1)}, f32[1,1024]{1,0:T(1,128)}, u32[]{:S(2)}) %copy-start.6) | copy-done | bytes 4120
  7.0 0.0 copy-start.7
  7.0 0.7 copy-done.7
  7.7 57.2 %adjoint_steps.1 = (f32[320,512]{1,0:T(8,128)S(1)}, f32[320,512]{1,0:T(8,128)S(1)}) custom-call(f32[320,512]{1,0:T(8,128)S(1)} %bitcast.10, f32[320,512]{1,0:T(8,128)S(1)} %bitcast.11, bf16[6,5,320,512]{3,2,1,0:T(8,128)(2,1)} %bitcast.13, bf16[5,320,512]{2,1,0:T(8,128)(2,1)S(1)} %bitcast.7, s32[6,512]{1,0:T(8,128)S(1)} %bitcast.12, s32[1,8]{1,0:T(1,128)S(1)} %copy-done.7, ...), custom_call_target="tpu_custom_call" | custom-call | tf_op jit(solution)/shard_map/adjoint_steps/pallas_call | solution.py:353
  64.9 0.8 %copy.13 = f32[512,320]{0,1:T(8,128)} copy(f32[512,320]{0,1:T(8,128)S(1)} %bitcast.9) | data formatting | bytes 1310720
  65.8 0.8 %copy.14 = f32[512,320]{0,1:T(8,128)} copy(f32[512,320]{0,1:T(8,128)S(1)} %bitcast.8) | data formatting | bytes 1310720
Async XLA Ops:
  0.6 1.4 %copy-start = (bf16[512,5,320]{0,2,1:T(8,128)(2,1)S(1)}, bf16[512,5,320]{0,2,1:T(8,128)(2,1)}, u32[]{:S(2)}) copy-start(bf16[512,5,320]{0,2,1:T(8,128)(2,1)} %param.12) | copy-start | bytes 4915204
  2.1 1.1 %copy-start.1 = (f32[512,320]{0,1:T(8,128)S(1)}, f32[512,320]{0,1:T(8,128)}, u32[]{:S(2)}) copy-start(f32[512,320]{0,1:T(8,128)} %param.9) | copy-start | bytes 1966084
  3.2 1.1 %copy-start.2 = (f32[512,320]{0,1:T(8,128)S(1)}, f32[512,320]{0,1:T(8,128)}, u32[]{:S(2)}) copy-start(f32[512,320]{0,1:T(8,128)} %param.10) | copy-start | bytes 1966084
  4.2 0.7 %copy-start.3 = (s32[512,6]{0,1:T(8,128)S(1)}, s32[512,6]{0,1:T(8,128)}, u32[]{:S(2)}) copy-start(s32[512,6]{0,1:T(8,128)} %param.13) | copy-start | bytes 36868
  5.0 0.7 %copy-start.4 = (s32[1,1024]{1,0:T(1,128)S(1)}, s32[1,1024]{1,0:T(1,128)}, u32[]{:S(2)}) copy-start(s32[1,1024]{1,0:T(1,128)} %fsrc_hbm.1) | copy-start | bytes 12292
  5.6 0.7 %copy-start.5 = (s32[1,1024]{1,0:T(1,128)S(1)}, s32[1,1024]{1,0:T(1,128)}, u32[]{:S(2)}) copy-start(s32[1,1024]{1,0:T(1,128)} %fdst_hbm.1) | copy-start | bytes 12292
  6.3 0.7 %copy-start.6 = (f32[1,1024]{1,0:T(1,128)S(1)}, f32[1,1024]{1,0:T(1,128)}, u32[]{:S(2)}) copy-start(f32[1,1024]{1,0:T(1,128)} %fw_hbm.1) | copy-start | bytes 12292
  7.0 0.7 copy-start.7

commit v2 on v1

--- a/solution.py
+++ b/solution.py
@@ -14,6 +14,8 @@
 SLOTS = 6
 RIM = 8
 CAP = 8
+GROUPS = 4
+GROUP = 32
 BODIES = 8
 BLKS = 16
 DEVS = 128
@@ -37,15 +39,19 @@
 
 def split(x):
     hi = x.astype(BF16)
-    return hi, (x - hi.astype(F32)).astype(BF16)
+    return jnp.concatenate([hi, (x - hi.astype(F32)).astype(BF16)], axis=0)
+
+
+def fold(y):
+    return y[: y.shape[0] // 2] + y[y.shape[0] // 2 :]
 
 
 def dot(a, b):
-    return jnp.dot(a, b, preferred_element_type=F32)
+    return fold(jnp.dot(a, b, preferred_element_type=F32))
 
 
 def dot_t(a, b):
-    return lax.dot_general(a, b, (((1,), (1,)), ((), ())), preferred_element_type=F32)
+    return fold(lax.dot_general(a, b, (((1,), (1,)), ((), ())), preferred_element_type=F32))
 
 
 def device(o):
@@ -53,22 +59,23 @@
 
 
 def kernel(
-    psi_hbm, src_hbm, coup_hbm, dinv_hbm, nbr_hbm, perm, fsrc_hbm, fdst_hbm, fw_hbm,
+    psi_hbm, src_hbm, coup_hbm, dinv_hbm, nbr_hbm, perm_hbm, fsrc_hbm, fdst_hbm, fw_hbm,
     adj_hbm, res_hbm,
-    psi, src, coup, dinv, nbr, fsrc, fdst, fw,
+    psi, src, coup, dinv, nbr, perm, fsrc, fdst, fw,
     sel, tab, near_hot, const, rim_hot,
-    halves, halo, near, base, fringe, inc_t, prec,
+    halves, halo, near, base, fringe, prec,
     out, inc, sums, total,
     lsem, ssem, rsem, rim_ssem, rim_rsem, sum_ssem, sum_rsem,
 ):
     b, k = lax.axis_index("body"), lax.axis_index("blk")
     me = b * BLKS + k
+    group = lax.div(me, GROUP)
     nxt, prv = lax.rem(k + 1, BLKS), lax.rem(k + BLKS - 1, BLKS)
 
     loads = [
         pltpu.make_async_copy(s, d, lsem.at[i])
         for i, (s, d) in enumerate(
-            [(psi_hbm, psi), (fsrc_hbm, fsrc), (nbr_hbm, nbr), (fdst_hbm, fdst), (fw_hbm, fw),
+            [(psi_hbm, psi), (fsrc_hbm, fsrc), (nbr_hbm, nbr), (perm_hbm, perm), (fdst_hbm, fdst), (fw_hbm, fw),
              (src_hbm, src), (dinv_hbm, dinv), (coup_hbm, coup)]
         )
     ]
@@ -89,9 +96,9 @@
 
     def halve(c):
         for v in range(VARS):
-            hi, lo = split(psi[v * CELLS + c * CC : v * CELLS + (c + 1) * CC, :])
-            halves[c, 0, v * CC : (v + 1) * CC, :] = hi
-            halves[c, 1, v * CC : (v + 1) * CC, :] = lo
+            both = split(psi[v * CELLS + c * CC : v * CELLS + (c + 1) * CC, :])
+            halves[c, v * CC : (v + 1) * CC, :] = both[:CC]
+            halves[c, CU + v * CC : CU + (v + 1) * CC, :] = both[CC:]
 
     def pack(y):
         n = y.shape[1]
@@ -112,7 +119,7 @@
         return jnp.concatenate([top, low], axis=0)
 
     def rims(s, c):
-        y = dot(halves[c, 0], const[...]) + dot(halves[c, 1], const[...])
+        y = dot(halves[c], const[...])
         halo[c] = y[:, LANES:]
         main, rest = pack(y[:, :LANES])
         out[s, c, DEVS : DEVS + 2, 0:8] = main[:2]
@@ -131,7 +138,7 @@
     def donors(s, c):
         def block(t, carry):
             cols = pl.ds(pl.multiple_of(t * 256, 256), 256)
-            y = dot(halves[c, 0], sel[:, cols]) + dot(halves[c, 1], sel[:, cols])
+            y = dot(halves[c], sel[:, cols])
             main, rest = pack(y)
             out[s, c, pl.ds(t * 32, 32), 0:8] = main
             out[s, c, pl.ds(t * 32, 32), 8:16] = rest
@@ -140,16 +147,20 @@
         lax.fori_loop(0, 4, block, 0)
         inc[s, c, pl.ds(me, 1)] = out[s, c, pl.ds(me, 1)]
 
-    def send(s, c):
+    def send_rims(s, c):
         for r in rim_copies(s, c):
             r.start()
 
+    def send_to(s, c, i):
+        o = lax.rem(me + i, DEVS)
+        pltpu.make_async_remote_copy(
+            slab(out, s, c, o, 1), slab(inc, s, c, me, 1), ssem.at[s, c], rsem.at[s, c, group],
+            device_id=device(o), device_id_type=MESH,
+        ).start()
+
+    def send(s, c):
         def one(i, carry):
-            o = lax.rem(me + lax.rem(i * 37, DEVS), DEVS)
-            pltpu.make_async_remote_copy(
-                slab(out, s, c, o, 1), slab(inc, s, c, me, 1), ssem.at[s, c], rsem.at[s, c],
-                device_id=device(o), device_id_type=MESH,
-            ).start()
+            send_to(s, c, i)
             return carry
 
         lax.fori_loop(1, DEVS, one, 0)
@@ -158,9 +169,9 @@
         for r in rim_copies(s, c):
             r.wait_recv()
 
-    def wait_fringe(s, c):
-        ref = slab(inc, s, c, 0, DEVS - 1)
-        pltpu.make_async_copy(ref, ref, rsem.at[s, c]).wait()
+    def wait_group(s, c, g, count):
+        ref = slab(inc, s, c, 0, count)
+        pltpu.make_async_copy(ref, ref, rsem.at[s, c, g]).wait()
 
     def wait_sends(s, c):
         ref = slab(out, s, c, 0, DEVS - 1)
@@ -168,13 +179,12 @@
         for r in rim_copies(s, c):
             r.wait_send()
 
-    def couple(s, c):
+    def couple(s, c, sends=None):
         wait_rims(s, c)
         zero = jnp.zeros((14, CAP, LANES), F32)
         main = jnp.concatenate([inc[s, c, DEVS : DEVS + 2, 0:8], zero], axis=0)
         rest = jnp.concatenate([inc[s, c, DEVS : DEVS + 2, 8:16], zero], axis=0)
-        hi, lo = split(unpack(main, rest))
-        edge = halo[c] + (dot(hi, rim_hot[...]) + dot(lo, rim_hot[...]))
+        edge = halo[c] + dot(split(unpack(main, rest)), rim_hot[...])
         lane = iota((1, LANES), 1)
         turn_lo = (lane < RIM) & (k == 0)
         turn_hi = (lane >= 56) & (lane < 64) & (k == BLKS - 1)
@@ -185,39 +195,51 @@
         edge = jnp.concatenate(
             [edge[: 2 * CC], cosine * e2 - sine * e3, sine * e2 + cosine * e3, edge[4 * CC :]], axis=0
         )
-        ehi, elo = split(edge)
+        edge = split(edge)
 
         def tile(t, carry):
             cols = pl.ds(pl.multiple_of(t * LANES, LANES), LANES)
-            ahi = jnp.concatenate([halves[c, 0, :, cols], ehi], axis=1)
-            alo = jnp.concatenate([halves[c, 1, :, cols], elo], axis=1)
-            near[...] = dot(ahi, near_hot[t]) + dot(alo, near_hot[t])
+            near[...] = dot(jnp.concatenate([halves[c, :, cols], edge], axis=1), near_hot[t])
+            if sends:
+                send_to(*sends, t * GROUP + 1)
             acc = jnp.zeros((VARS, CC, LANES), F32)
             for v in range(VARS):
                 rows = slice(v * CELLS + c * CC, v * CELLS + (c + 1) * CC)
                 for m in range(SLOTS):
+                    if sends:
+                        send_to(*sends, t * GROUP + 2 + v * SLOTS + m)
                     x = near[v * CC : (v + 1) * CC, m * LANES : (m + 1) * LANES]
                     acc = acc + coup[m, :, rows, cols].astype(F32) * x[None]
             for v in range(VARS):
                 rows = slice(v * CELLS + c * CC, v * CELLS + (c + 1) * CC)
                 base[c, v * CC : (v + 1) * CC, cols] = src[rows, cols] - psi[rows, cols] + acc[v]
+            if sends:
+
+                @pl.when(t < TILES - 1)
+                def _():
+                    send_to(*sends, t * GROUP + GROUP)
+
             return carry
 
         lax.fori_loop(0, TILES, tile, 0)
 
     def gather_fringe(s, c):
-        wait_fringe(s, c)
-
-        def block(t, carry):
-            cols = pl.ds(pl.multiple_of(t * 256, 256), 256)
-            x = unpack(inc[s, c, pl.ds(t * 32, 32), 0:8], inc[s, c, pl.ds(t * 32, 32), 8:16])
-            hi, lo = split(x * fw[:, cols])
-            inc_t[0, :, cols] = hi
-            inc_t[1, :, cols] = lo
+        def block(g):
+            cols = pl.ds(pl.multiple_of(g * 256, 256), 256)
+            x = unpack(inc[s, c, pl.ds(g * GROUP, GROUP), 0:8], inc[s, c, pl.ds(g * GROUP, GROUP), 8:16])
+            return dot_t(split(x * fw[:, cols]), tab[:, cols])
+
+        fringe[...] = jnp.zeros_like(fringe)
+
+        def other(i, carry):
+            g = lax.rem(group + GROUPS - i, GROUPS)
+            wait_group(s, c, g, GROUP)
+            fringe[...] += block(g)
             return carry
 
-        lax.fori_loop(0, 4, block, 0)
-        fringe[...] = dot_t(inc_t[0], tab[...]) + dot_t(inc_t[1], tab[...])
+        lax.fori_loop(1, GROUPS, other, 0)
+        wait_group(s, c, group, GROUP - 1)
+        fringe[...] += block(group)
 
     def residual(s, c, square):
         def tile(t, square):
@@ -228,14 +250,13 @@
                 own = slice(v * CC, (v + 1) * CC)
                 r = base[c, own, cols] + fringe[own, cols]
                 square = square + jnp.sum((r * r).reshape(CC // 8, 8, LANES), axis=0)
-                acc = acc + dinv[:, rows, cols].astype(F32) * r[None]
                 if s == STEPS - 1:
                     src[rows, cols] = r
-            for v in range(VARS):
-                rows = slice(v * CELLS + c * CC, v * CELLS + (c + 1) * CC)
-                if s == STEPS - 1:
-                    prec[rows, cols] = acc[v]
                 else:
+                    acc = acc + dinv[:, rows, cols].astype(F32) * r[None]
+            if s < STEPS - 1:
+                for v in range(VARS):
+                    rows = slice(v * CELLS + c * CC, v * CELLS + (c + 1) * CC)
                     psi[rows, cols] = psi[rows, cols] + CFL * acc[v]
             return square
 
@@ -263,14 +284,14 @@
     rims(0, 0)
     donors(0, 0)
     pl.semaphore_wait(bar, DEVS - 1)
+    send_rims(0, 0)
     send(0, 0)
-    for c in range(1, CHUNKS):
-        halve(c)
-        rims(0, c)
-        donors(0, c)
-        send(0, c)
-
-    for c in loads[2:5]:
+    halve(1)
+    rims(0, 1)
+    send_rims(0, 1)
+    donors(0, 1)
+
+    for c in loads[2:6]:
         c.wait()
 
     def build_in(i, carry):
@@ -295,21 +316,23 @@
         hot = jnp.where((row == low) & (col == j), 1.0, hot)
         hot = jnp.where((row == RIM + j) & (col == high), 1.0, hot)
     rim_hot[...] = hot.astype(BF16)
-    for c in loads[5:]:
+    for c in loads[6:]:
         c.wait()
 
     square = [jnp.zeros((8, LANES), F32) for _ in range(STEPS)]
-    for s in range(STEPS):
-        for c in range(CHUNKS):
-            couple(s, c)
-        for c in range(CHUNKS):
-            gather_fringe(s, c)
-            square[s] = residual(s, c, square[s])
-            if s < STEPS - 1:
-                halve(c)
-                rims(s + 1, c)
-                donors(s + 1, c)
-                send(s + 1, c)
+    order = [(s, c) for s in range(STEPS) for c in range(CHUNKS)]
+    pending = (0, 1)
+    for s, c in order:
+        couple(s, c, pending)
+        pending = None
+        gather_fringe(s, c)
+        square[s] = residual(s, c, square[s])
+        if s < STEPS - 1:
+            halve(c)
+            rims(s + 1, c)
+            send_rims(s + 1, c)
+            donors(s + 1, c)
+            pending = (s + 1, c)
 
     sums[...] = jnp.concatenate([jnp.sum(x, axis=0, keepdims=True) for x in square], axis=0)[None]
     total[pl.ds(me, 1)] = sums[...]
@@ -324,6 +347,19 @@
     lax.fori_loop(1, DEVS, tell, 0)
     res = pltpu.make_async_copy(src, res_hbm, lsem.at[0])
     res.start()
+
+    def precondition(i, carry):
+        c, t = lax.div(i, TILES), lax.rem(i, TILES)
+        cols = pl.ds(pl.multiple_of(t * LANES, LANES), LANES)
+        acc = jnp.zeros((VARS, CC, LANES), F32)
+        for v in range(VARS):
+            rows = pl.ds(pl.multiple_of(v * CELLS + c * CC, CC), CC)
+            acc = acc + dinv[:, rows, cols].astype(F32) * src[rows, cols][None]
+        for v in range(VARS):
+            prec[pl.ds(pl.multiple_of(v * CELLS + c * CC, CC), CC), cols] = acc[v]
+        return carry
+
+    lax.fori_loop(0, CHUNKS * TILES, precondition, 0)
     ref = total.at[pl.ds(0, DEVS - 1)]
     pltpu.make_async_copy(ref, ref, sum_rsem).wait()
     q = jnp.sum(jnp.sum(total[...], axis=0), axis=1, keepdims=True) * (1.0 / TOTAL) + 1e-06
@@ -353,7 +389,7 @@
     adjoint, residual = pl.pallas_call(
         kernel,
         out_shape=[jax.ShapeDtypeStruct((BW, NB), F32)] * 2,
-        in_specs=[any_space] * 5 + [pl.BlockSpec(memory_space=pltpu.SMEM)] + [any_space] * 3,
+        in_specs=[any_space] * 9,
         out_specs=[any_space] * 2,
         scratch_shapes=[
             vmem((BW, NB), F32),
@@ -361,6 +397,7 @@
             vmem((SLOTS, VARS, BW, NB), BF16),
             vmem((VARS, BW, NB), BF16),
             vmem((SLOTS, NB), jnp.int32),
+            pltpu.SMEM((1, RIM), jnp.int32),
             vmem((1, slots), jnp.int32),
             vmem((1, slots), jnp.int32),
             vmem((1, slots), F32),
@@ -369,32 +406,31 @@
             vmem((TILES, 2 * LANES, SLOTS * LANES), BF16),
             vmem((NB, 2 * LANES), BF16),
             vmem((LANES, LANES), BF16),
-            vmem((CHUNKS, 2, CU, NB), BF16),
+            vmem((CHUNKS, 2 * CU, NB), BF16),
             vmem((CHUNKS, CU, LANES), F32),
             vmem((CU, SLOTS * LANES), F32),
             vmem((CHUNKS, CU, NB), F32),
             vmem((CU, NB), F32),
-            vmem((2, CU, slots), BF16),
             vmem((BW, NB), F32),
             vmem((STEPS, CHUNKS, DEVS + 2, 16, LANES), F32),
             vmem((STEPS, CHUNKS, DEVS + 2, 16, LANES), F32),
             vmem((1, STEPS, LANES), F32),
             vmem((DEVS, STEPS, LANES), F32),
-            dma((8,)),
+            dma((9,)),
             dma((STEPS, CHUNKS)),
-            dma((STEPS, CHUNKS)),
+            dma((STEPS, CHUNKS, GROUPS)),
             dma((STEPS, CHUNKS, 2)),
             dma((STEPS, CHUNKS, 2)),
             dma,
             dma,
         ],
         compiler_params=pltpu.CompilerParams(
-            collective_id=0, has_side_effects=True, vmem_limit_bytes=48 << 20
+            collective_id=0, has_side_effects=True, vmem_limit_bytes=40 << 20
         ),
         name="adjoint_steps",
     )(
-        psi.T, source.T, coupling.transpose(1, 2, 3, 0), diag_inv.transpose(1, 2, 0), neighbours.T,
-        seam_perm, fringe_src, fringe_dst, fringe_weight,
+        *[pltpu.with_memory_space_constraint(x, pltpu.HBM) for x in (psi.T, source.T, coupling.transpose(1, 2, 3, 0), diag_inv.transpose(1, 2, 0), neighbours.T,
+        seam_perm, fringe_src, fringe_dst, fringe_weight)]
     )
     return adjoint.T, residual.T
 

time: 67 us -> 56.7 us (0.85)
  local copies, waits for them, and re-layouts: 8.7 us -> 1.67 us
  Pallas kernels: 57.2 us -> 54.3 us
    unnamed x18 -> x2, local copies, waits for them, and re-layouts: 8.7 us -> 1.67 us
    pallas_call x1, Pallas kernels: 57.2 us -> 54.3 us  [shards(): pl.pallas_call(kernel, out_shape=[jax.ShapeDtypeStruct((BW, NB), F32)] *...]
where the time goes in v2:
time: 56.7 us; the launch traced here: 56.6 us
  Pallas kernels  54.3 us (96%)
  local copies, waits for them, and re-layouts  1.67 us (3%)
  between operations  0.64 us (1%)
    pallas_call x1, Pallas kernels, shards(): pl.pallas_call(kernel, out_shape=[jax.ShapeDtypeStruct((BW, NB), F32)] *...  54.3 us
    unnamed x2, local copies, waits for them, and re-layouts  1.67 us

profile of v2, /device:TPU:1, one launch (start us, length us, event | category | flops | bytes accessed | tf_op | source)
XLA Modules:
  0.0 56.6 jit_solution(2621169326321702333)
XLA Ops:
  0.6 54.3 %adjoint_steps.1 = (f32[320,512]{1,0:T(8,128)S(1)}, f32[320,512]{1,0:T(8,128)S(1)}) custom-call(f32[320,512]{1,0:T(8,128)} %bitcast.11, f32[320,512]{1,0:T(8,128)} %bitcast.12, bf16[6,5,320,512]{3,2,1,0:T(8,128)(2,1)} %bitcast.9, bf16[5,320,512]{2,1,0:T(8,128)(2,1)} %bitcast.10, s32[6,512]{1,0:T(8,128)} %bitcast.13, s32[1,8]{1,0:T(1,128)} %perm_hbm.1, ...), custom_call_target="tpu_custom_call" | custom-call | tf_op jit(solution)/shard_map/adjoint_steps/pallas_call | solution.py:389
  54.9 0.8 %copy.13 = f32[512,320]{0,1:T(8,128)} copy(f32[512,320]{0,1:T(8,128)S(1)} %bitcast.8) | data formatting | bytes 1310720
  55.7 0.8 %copy.14 = f32[512,320]{0,1:T(8,128)} copy(f32[512,320]{0,1:T(8,128)S(1)} %bitcast.7) | data formatting | bytes 1310720

commit v3 on v2

--- a/solution.py
+++ b/solution.py
@@ -58,17 +58,28 @@
     return (lax.div(o, BLKS), lax.rem(o, BLKS))
 
 
+def far_first(b, k):
+    y, core, z, x = lax.div(b, 2), lax.rem(b, 2), lax.div(k, 4), lax.rem(k, 4)
+    bodies = {(i, j): lax.rem(y + i, 4) * 2 + lax.rem(core + j, 2) for i in range(4) for j in range(2)}
+    blks = {(i, j): lax.rem(z + i, 4) * 4 + lax.rem(x + j, 4) for i in range(4) for j in range(4)}
+    steps = [(p, q) for p in bodies for q in blks if any(p + q)]
+    hops = (0, 1, 2, 1)
+    steps.sort(key=lambda s: -(hops[s[0][0]] + hops[s[1][0]] + hops[s[1][1]]))
+    return [(bodies[p], blks[q]) for p, q in steps]
+
+
 def kernel(
     psi_hbm, src_hbm, coup_hbm, dinv_hbm, nbr_hbm, perm_hbm, fsrc_hbm, fdst_hbm, fw_hbm,
-    adj_hbm, res_hbm,
+    results,
     psi, src, coup, dinv, nbr, perm, fsrc, fdst, fw,
     sel, tab, near_hot, const, rim_hot,
     halves, halo, near, base, fringe, prec,
     out, inc, sums, total,
-    lsem, ssem, rsem, rim_ssem, rim_rsem, sum_ssem, sum_rsem,
+    lsem, ssem, rsem, rim_ssem, rim_rsem, sum_ssem, sum_rsem, row_sem,
 ):
     b, k = lax.axis_index("body"), lax.axis_index("blk")
     me = b * BLKS + k
+    adj, res = results.at[0], results.at[1]
     group = lax.div(me, GROUP)
     nxt, prv = lax.rem(k + 1, BLKS), lax.rem(k + BLKS - 1, BLKS)
 
@@ -84,12 +95,19 @@
 
     bar = pltpu.get_barrier_semaphore()
 
-    def greet(i, carry):
-        o = lax.rem(me + i, DEVS)
-        pl.semaphore_signal(bar, inc=1, device_id=device(o), device_id_type=MESH)
+    def greet_row(i, carry):
+        pl.semaphore_signal(bar, inc=1, device_id=(b, lax.rem(k + i, BLKS)), device_id_type=MESH)
         return carry
 
-    lax.fori_loop(1, DEVS, greet, 0)
+    def tell_column(sem):
+        def one(i, carry):
+            pl.semaphore_signal(sem, inc=1, device_id=(lax.rem(b + i, BODIES), k), device_id_type=MESH)
+            return carry
+
+        lax.fori_loop(1, BODIES, one, 0)
+
+    lax.fori_loop(1, BLKS, greet_row, 0)
+    tell_column(bar)
 
     def slab(ref, s, c, first, count):
         return ref.at[s, c, pl.ds(first, count), pl.ds(0, ROWS)]
@@ -251,7 +269,7 @@
                 r = base[c, own, cols] + fringe[own, cols]
                 square = square + jnp.sum((r * r).reshape(CC // 8, 8, LANES), axis=0)
                 if s == STEPS - 1:
-                    src[rows, cols] = r
+                    res[rows, cols] = r
                 else:
                     acc = acc + dinv[:, rows, cols].astype(F32) * r[None]
             if s < STEPS - 1:
@@ -281,9 +299,11 @@
         return carry
 
     lax.fori_loop(0, NB // 64, build, 0)
+    pl.semaphore_wait(bar, BLKS - 1 + BODIES - 1)
+    tell_column(row_sem)
     rims(0, 0)
     donors(0, 0)
-    pl.semaphore_wait(bar, DEVS - 1)
+    pl.semaphore_wait(row_sem, BODIES - 1)
     send_rims(0, 0)
     send(0, 0)
     halve(1)
@@ -337,16 +357,10 @@
     sums[...] = jnp.concatenate([jnp.sum(x, axis=0, keepdims=True) for x in square], axis=0)[None]
     total[pl.ds(me, 1)] = sums[...]
 
-    def tell(i, carry):
-        o = lax.rem(me + i, DEVS)
+    for to in far_first(b, k):
         pltpu.make_async_remote_copy(
-            sums.at[0], total.at[me], sum_ssem, sum_rsem, device_id=device(o), device_id_type=MESH
+            sums.at[0], total.at[me], sum_ssem, sum_rsem, device_id=to, device_id_type=MESH
         ).start()
-        return carry
-
-    lax.fori_loop(1, DEVS, tell, 0)
-    res = pltpu.make_async_copy(src, res_hbm, lsem.at[0])
-    res.start()
 
     def precondition(i, carry):
         c, t = lax.div(i, TILES), lax.rem(i, TILES)
@@ -354,7 +368,7 @@
         acc = jnp.zeros((VARS, CC, LANES), F32)
         for v in range(VARS):
             rows = pl.ds(pl.multiple_of(v * CELLS + c * CC, CC), CC)
-            acc = acc + dinv[:, rows, cols].astype(F32) * src[rows, cols][None]
+            acc = acc + dinv[:, rows, cols].astype(F32) * res[rows, cols][None]
         for v in range(VARS):
             prec[pl.ds(pl.multiple_of(v * CELLS + c * CC, CC), CC), cols] = acc[v]
         return carry
@@ -367,18 +381,14 @@
 
     def last(i, carry):
         rows = pl.ds(pl.multiple_of(i * 32, 32), 32)
-        psi[rows] = psi[rows] + cfl * prec[rows]
+        adj[rows] = psi[rows] + cfl * prec[rows]
         return carry
 
     lax.fori_loop(0, BW // 32, last, 0)
-    adj = pltpu.make_async_copy(psi, adj_hbm, lsem.at[1])
-    adj.start()
     pltpu.make_async_copy(ref, ref, sum_ssem).wait()
     for s in range(STEPS):
         for c in range(CHUNKS):
             wait_sends(s, c)
-    res.wait()
-    adj.wait()
 
 
 def shards(psi, source, coupling, diag_inv, neighbours, seam_perm, fringe_src, fringe_dst, fringe_weight):
@@ -386,11 +396,11 @@
     vmem = pltpu.VMEM
     dma = pltpu.SemaphoreType.DMA
     slots = DEVS * CAP
-    adjoint, residual = pl.pallas_call(
+    results = pl.pallas_call(
         kernel,
-        out_shape=[jax.ShapeDtypeStruct((BW, NB), F32)] * 2,
+        out_shape=jax.ShapeDtypeStruct((2, BW, NB), F32),
         in_specs=[any_space] * 9,
-        out_specs=[any_space] * 2,
+        out_specs=pl.BlockSpec(memory_space=vmem),
         scratch_shapes=[
             vmem((BW, NB), F32),
             vmem((BW, NB), F32),
@@ -423,6 +433,7 @@
             dma((STEPS, CHUNKS, 2)),
             dma,
             dma,
+            pltpu.SemaphoreType.REGULAR,
         ],
         compiler_params=pltpu.CompilerParams(
             collective_id=0, has_side_effects=True, vmem_limit_bytes=40 << 20
@@ -432,7 +443,7 @@
         *[pltpu.with_memory_space_constraint(x, pltpu.HBM) for x in (psi.T, source.T, coupling.transpose(1, 2, 3, 0), diag_inv.transpose(1, 2, 0), neighbours.T,
         seam_perm, fringe_src, fringe_dst, fringe_weight)]
     )
-    return adjoint.T, residual.T
+    return results[0].T, results[1].T
 
 
 def solution(mesh):

time: 56.7 us -> 55.1 us (0.972)
  Pallas kernels: 54.3 us -> 53.2 us
    unnamed x2 -> x0, local copies, waits for them, and re-layouts: 1.67 us -> none
    transpose x0 -> x1, local copies, waits for them, and re-layouts: none -> 1.15 us  [shards(): return (results[0].T, results[1].T)]
    pallas_call x1, Pallas kernels: 54.3 us -> 53.2 us  [shards(): pl.pallas_call(kernel, out_shape=jax.ShapeDtypeStruct((2, BW, NB), F32),...]
where the time goes in v3:
time: 55.1 us; the launch traced here: 55 us
  Pallas kernels  53.2 us (97%)
  local copies, waits for them, and re-layouts  1.15 us (2%)
  between operations  0.64 us (1%)
    pallas_call x1, Pallas kernels, shards(): pl.pallas_call(kernel, out_shape=jax.ShapeDtypeStruct((2, BW, NB), F32),...  53.2 us
    transpose x1, local copies, waits for them, and re-layouts, shards(): return (results[0].T, results[1].T)  1.15 us

profile of v3, /device:TPU:1, one launch (start us, length us, event | category | flops | bytes accessed | tf_op | source)
XLA Modules:
  0.0 55.0 jit_solution(8218026818600503804)
XLA Ops:
  0.6 53.2 %adjoint_steps.1 = f32[2,320,512]{2,1,0:T(8,128)S(1)} custom-call(f32[320,512]{1,0:T(8,128)} %bitcast.15, f32[320,512]{1,0:T(8,128)} %bitcast.16, bf16[6,5,320,512]{3,2,1,0:T(8,128)(2,1)} %bitcast.13, bf16[5,320,512]{2,1,0:T(8,128)(2,1)} %bitcast.14, s32[6,512]{1,0:T(8,128)} %bitcast.17, s32[1,8]{1,0:T(1,128)} %perm_hbm.1, s32[1,1024]{1,0:T(1,128)} %fsrc_hbm.1, ...), custom_call_target="tpu_custom_call" | custom-call | tf_op jit(solution)/shard_map/adjoint_steps/pallas_call | solution.py:399
  53.8 1.1 %slice_bitcast_fusion = (f32[512,320]{0,1:T(8,128)}, f32[512,320]{0,1:T(8,128)}) fusion(f32[2,320,512]{2,1,0:T(8,128)S(1)} %adjoint_steps.1), kind=kLoop, calls=%fused_computation | loop fusion | bytes 2621440 | tf_op jit(solution)/shard_map/transpose | solution.py:446

commit v4 on v3

--- a/solution.py
+++ b/solution.py
@@ -170,10 +170,11 @@
             r.start()
 
     def send_to(s, c, i):
-        o = lax.rem(me + i, DEVS)
+        o = me + i
+        o = jnp.where(o >= DEVS, o - DEVS, o)
         pltpu.make_async_remote_copy(
             slab(out, s, c, o, 1), slab(inc, s, c, me, 1), ssem.at[s, c], rsem.at[s, c, group],
-            device_id=device(o), device_id_type=MESH,
+            device_id=o, device_id_type=pl.DeviceIdType.LOGICAL,
         ).start()
 
     def send(s, c):
@@ -247,15 +248,16 @@
             x = unpack(inc[s, c, pl.ds(g * GROUP, GROUP), 0:8], inc[s, c, pl.ds(g * GROUP, GROUP), 8:16])
             return dot_t(split(x * fw[:, cols]), tab[:, cols])
 
-        fringe[...] = jnp.zeros_like(fringe)
-
         def other(i, carry):
             g = lax.rem(group + GROUPS - i, GROUPS)
             wait_group(s, c, g, GROUP)
             fringe[...] += block(g)
             return carry
 
-        lax.fori_loop(1, GROUPS, other, 0)
+        before = lax.rem(group + GROUPS - 1, GROUPS)
+        wait_group(s, c, before, GROUP)
+        fringe[...] = block(before)
+        lax.fori_loop(2, GROUPS, other, 0)
         wait_group(s, c, group, GROUP - 1)
         fringe[...] += block(group)
 

time: 55.1 us -> 55.1 us (level)
  no operation moved by 1% of the time
where the time goes in v4:
time: 55.1 us; the launch traced here: 55 us
  Pallas kernels  53.3 us (97%)
  local copies, waits for them, and re-layouts  1.15 us (2%)
  between operations  0.64 us (1%)
    pallas_call x1, Pallas kernels, shards(): pl.pallas_call(kernel, out_shape=jax.ShapeDtypeStruct((2, BW, NB), F32),...  53.3 us
    transpose x1, local copies, waits for them, and re-layouts, shards(): return (results[0].T, results[1].T)  1.15 us

profile of v4, /device:TPU:1, one launch (start us, length us, event | category | flops | bytes accessed | tf_op | source)
XLA Modules:
  0.0 55.0 jit_solution(7324276859753634131)
XLA Ops:
  0.6 53.3 %adjoint_steps.1 = f32[2,320,512]{2,1,0:T(8,128)S(1)} custom-call(f32[320,512]{1,0:T(8,128)} %bitcast.15, f32[320,512]{1,0:T(8,128)} %bitcast.16, bf16[6,5,320,512]{3,2,1,0:T(8,128)(2,1)} %bitcast.13, bf16[5,320,512]{2,1,0:T(8,128)(2,1)} %bitcast.14, s32[6,512]{1,0:T(8,128)} %bitcast.17, s32[1,8]{1,0:T(1,128)} %perm_hbm.1, s32[1,1024]{1,0:T(1,128)} %fsrc_hbm.1, ...), custom_call_target="tpu_custom_call" | custom-call | tf_op jit(solution)/shard_map/adjoint_steps/pallas_call | solution.py:401
  53.9 1.1 %slice_bitcast_fusion = (f32[512,320]{0,1:T(8,128)}, f32[512,320]{0,1:T(8,128)}) fusion(f32[2,320,512]{2,1,0:T(8,128)S(1)} %adjoint_steps.1), kind=kLoop, calls=%fused_computation | loop fusion | bytes 2621440 | tf_op jit(solution)/shard_map/transpose | solution.py:448
